TPU v7x, 32 devices: a whole 2x2x4 slice. The times are simulated.
32 devices in a mesh: face: 2 (over x), rows: 16 (over z, y, core).
Axes of the slice: x: 2, y: 2, z: 4, core: 2. Of those that a mesh axis runs over, the one named last changes fastest.
Arguments:
- final_adjoint: float32 [16, 6, 256, 256], P(None, 'face', 'rows'), may hold values from -6 to 6
- courant_x: float32 [16, 6, 256, 256], P(None, 'face', 'rows'), may hold values from 0.05 to 0.45
- courant_y: float32 [16, 6, 256, 256], P(None, 'face', 'rows'), may hold values from 0.05 to 0.45
- ray_tiles: bfloat16 [2, 1024, 16, 512], P('face', 'rows'), may hold values from -1.5 to 1.5
- ray_innov: bfloat16 [2, 1024, 16], P('face', 'rows'), may hold values from -6 to 6
- ray_dest: int32 [2, 1024, 1], P('face', 'rows'), may hold values from 0 to 15; in each aligned block of 64 rows (0 to 63, 64 to 127, ..., all dimensions but the last counted through in order) at most 8 rows name the same one
- ray_cols: int32 [2, 1024, 32], P('face', 'rows'), may hold values from 0 to 12287
Outputs:
- prior_adjoint: float32 [16, 6, 256, 256], P(None, 'face', 'rows')
Inputs may be any that keep to these rules, and one draw needn't show every extreme that they name: `ray_dest`: each device's 64 ray blocks name one band each, at most 8 blocks for one band; some device sends exactly 8 blocks to some band.
All inputs are finite; a program needn't handle non-finite values.
Results may differ from a plain program's by a relative error of at most 0.0003.
Values may be sent and summed in bfloat16 or wider, within the bound.
No kernel may reach another device: no remote copies, remote signals or barrier semaphores. Data moves between devices by JAX's collectives and lax.ppermute only.
A program may use at most 128 MiB of HBM per device.

v0:
```python
import jax
import jax.numpy as jnp
from jax import lax
from jax.sharding import PartitionSpec as P


def broadcast(value, axis, source):
    kept = jnp.where(lax.axis_index(axis) == source, value, 0).astype(value.dtype)
    return lax.psum(kept, axis)


def from_partner(block, axis, apart):
    count = lax.axis_size(axis)
    route = []
    for low in range(count):
        high = low | 1 << apart
        if high != low and high < count:
            route += [(low, high), (high, low)]
    return lax.ppermute(block, axis, route)


def shifted(value, axis, by):
    count = lax.axis_size(axis)
    return lax.ppermute(value, axis, [(i, (i + by) % count) for i in range(count)])


def spread(payload, band_id, band):
    whole_edge = broadcast(payload.astype(jnp.bfloat16), "rows", 0).astype(payload.dtype)
    return lax.dynamic_slice_in_dim(whole_edge, band_id * band, band, 2)


def trade(packet):
    return from_partner(packet.astype(jnp.bfloat16), "face", 0).astype(packet.dtype)


def transpose_step(adjoint, courant_x, courant_y):
    levels, faces, band, edge = adjoint.shape
    bands = lax.axis_size("rows")
    band_id = lax.axis_index("rows")
    first = lax.axis_index("face") == 0
    along = courant_x * adjoint
    upward = courant_y * adjoint
    result = (1.0 - courant_x - courant_y) * adjoint
    result = result + jnp.pad(along[..., 1:], ((0, 0), (0, 0), (0, 0), (0, 1)))
    result = result + jnp.pad(upward[:, :, 1:, :], ((0, 0), (0, 0), (0, 1), (0, 0)))
    side = along[..., 0]
    top_row = upward[:, :, 0, :]
    below = shifted(top_row, "rows", -1)
    zero_row = jnp.zeros_like(below[:, 0])
    seam_local = jnp.where(
        first,
        jnp.stack([zero_row, zero_row, below[:, 1]], axis=1),
        jnp.stack([zero_row, below[:, 0], zero_row], axis=1),
    )
    mirrored = top_row[..., ::-1]
    out_rot = jnp.where(first, mirrored[:, 2], mirrored[:, 1])
    loc_rot = jnp.where(first, mirrored[:, 0], zero_row)
    piece = spread(jnp.stack([out_rot, loc_rot], axis=1), band_id, band)
    received = trade(jnp.concatenate([piece[:, 0], side[:, 0], below[:, 2]], axis=-1))
    cross = received[:, :band]
    far_side = received[:, band : 2 * band]
    far_unrot = received[:, 2 * band :]
    local = piece[:, 1]
    zero_piece = jnp.zeros_like(cross)
    col_add = jnp.stack(
        [jnp.where(first, cross, zero_piece), jnp.where(first, zero_piece, cross), local], axis=1
    )
    zero_unrot = jnp.zeros_like(far_unrot)
    cross_unrot = jnp.stack(
        [jnp.where(first, far_unrot, zero_unrot), zero_unrot, zero_unrot], axis=1
    )
    bottom = jnp.where(band_id == bands - 1, seam_local + cross_unrot, below)
    right_col = jnp.concatenate([side[:, 1:, :], far_side[:, None, :]], axis=1)
    result = result.at[:, :, band - 1, :].add(bottom)
    result = result.at[:, :, :, 0].add(col_add)
    result = result.at[:, :, :, edge - 1].add(right_col)
    return result


def ray_forcing(ray_tiles, ray_innov, ray_dest, ray_cols, field_shape):
    tiles = ray_tiles[0]
    innov = ray_innov[0]
    target = ray_dest[0][:, 0]
    cells = ray_cols[0]
    bands = lax.axis_size("rows")
    blocks = tiles.shape[0]
    slots = max(2, 2 * blocks // bands)
    hits = (target[:, None] == jnp.arange(bands, dtype=jnp.int32)[None, :]).astype(jnp.int32)
    order = jnp.sum(jnp.cumsum(hits, axis=0) * hits, axis=1) - 1
    slot_id = target * slots + order
    cell_buf = jnp.zeros((bands * slots, cells.shape[1]), jnp.int32).at[slot_id].set(cells)
    cell_buf = cell_buf.reshape(bands, slots, cells.shape[1])
    cell_got = lax.all_to_all(cell_buf, "rows", split_axis=0, concat_axis=0, tiled=True)
    contrib = jnp.einsum("br,brk->bk", innov, tiles, preferred_element_type=jnp.float32)
    sum_buf = jnp.zeros((bands * slots, contrib.shape[1]), jnp.float32).at[slot_id].set(contrib)
    sum_buf = sum_buf.reshape(bands, slots, contrib.shape[1])
    sums = lax.all_to_all(sum_buf, "rows", split_axis=0, concat_axis=0, tiled=True)
    levels = field_shape[0]
    width = cell_got.shape[2]
    values = jnp.transpose(sums.reshape(-1, levels, width), (1, 0, 2)).reshape(levels, -1)
    total = field_shape[1] * field_shape[2] * field_shape[3]
    flat = jnp.zeros((levels, total), jnp.float32).at[:, cell_got.reshape(-1)].add(values)
    return flat.reshape(field_shape)


def per_device(final_adjoint, courant_x, courant_y, ray_tiles, ray_innov, ray_dest, ray_cols):
    forcing = ray_forcing(ray_tiles, ray_innov, ray_dest, ray_cols, final_adjoint.shape)
    mid_adjoint = transpose_step(final_adjoint, courant_x, courant_y) + forcing
    return transpose_step(mid_adjoint, courant_x, courant_y)


def solution(mesh):
    placed = (
        P(None, "face", "rows", None),
        P(None, "face", "rows", None),
        P(None, "face", "rows", None),
        P("face", "rows", None, None),
        P("face", "rows", None),
        P("face", "rows", None),
        P("face", "rows", None),
    )
    return jax.shard_map(
        per_device,
        mesh=mesh,
        in_specs=placed,
        out_specs=P(None, "face", "rows", None),
        check_vma=False,
    )
```

profile of v0, /device:TPU:0, one launch (start us, length us, event | category | flops | bytes accessed | tf_op | source)
XLA Modules:
  0.0 253.2 jit_solution(12293367904915491070)
XLA Ops:
  0.0 1.0 copy.283
  1.0 0.7 fusion.16
  1.8 0.8 select_reduce_fusion
  2.6 0.7 fusion.27
  3.3 0.8 scatter_custom_fusion
  4.1 0.7 reshape.332
  4.8 7.5 %all-to-all-start = ((s32[16,1,256]{2,1,0:T(1,128)}), s32[16,1,256]{2,1,0:T(1,128)}, u32[]{:S(2)}, u32[]{:S(2)}) async-start(s32[16,1,256]{2,1,0:T(1,128)} %reshape.332), calls=%async_computation | async-start | bytes 32768 | tf_op jit(solution)/shard_map/all_to_all | solution.py:93
  12.2 1.9 fusion.28
  14.1 0.6 copy.304
  14.8 4.3 %collective-permute-start = (f32[16,3,256]{2,0,1:T(8,128)}, f32[16,3,256]{2,0,1:T(8,128)}, u32[]{:S(2)}, u32[]{:S(2)}) collective-permute-start(f32[16,3,256]{2,0,1:T(8,128)} %bitcast.72), channel_id=1, source_target_pairs={{0,15},{1,0},{2,1},{3,2},{4,3},{5,4},{6,5},{7,6},{8,7},{9,8},{10,9... | collective-permute-start | bytes 147464 | tf_op jit(solution)/shard_map/ppermute | solution.py:24
  19.1 1.0 slice.335
  20.0 0.8 fusion.32
  20.8 1.2 slice.334
  22.6 57.9 %psum.14 = bf16[16,2,256]{2,0,1:T(8,128)(2,1)S(1)} all-reduce(bf16[16,2,256]{2,0,1:T(8,128)(2,1)S(1)} %maximum_select_fusion), channel_id=1, replica_groups=mesh['face'=2,'rows'=16] {'rows'}, use_global_device_ids=true, to_apply=%region_0.0 | all-reduce | flops 8192 | bytes 32768 | tf_op jit(solution)/shard_map/psum | solution.py:9
  80.6 0.6 fusion.23
  81.2 0.9 copy.279
  82.5 2.1 pad_add_fusion.1
  84.5 1.3 fusion.24
  85.8 0.6 slice.350
  86.4 0.7 slice.352
  87.1 1.6 scatter_custom_fusion.1
  88.7 4.2 %all-to-all-start.1 = ((f32[16,8,512]{2,1,0:T(8,128)}), f32[16,8,512]{2,1,0:T(8,128)}, u32[]{:S(2)}, u32[]{:S(2)}) async-start(f32[16,8,512]{2,1,0:T(8,128)} %bitcast.78), calls=%async_computation.1 | async-start | bytes 524288 | tf_op jit(solution)/shard_map/all_to_all | solution.py:97
  92.9 0.5 broadcast.202
  93.4 1.3 reduce.12
  95.0 0.7 fusion.21
  95.7 0.8 pad_maximum_fusion.4
  96.5 1.5 collective-permute-start.1
  98.0 0.7 fusion.31
  98.7 1.5 collective-permute-done.1
  100.3 0.8 fusion.11
  101.2 2.1 scatter-add.26
  103.3 0.7 maximum_bitcast_fusion
  104.0 1.1 copy.281
  105.1 1.8 slice_add_fusion.3
  106.9 3.0 %scatter-add.29 = f32[16,3,16,256]{3,2,1,0:T(8,128)S(1)} dynamic-update-slice(f32[16,3,16,256]{3,2,1,0:T(8,128)S(1)} %scatter-add.26, f32[16,3,16,1]{3,2,1,0:T(8,128)} %slice_add_fusion.3, s32[]{:T(128)} %constant.177.clone.1, s32[]{:T(128)} %constant.177.clone.1, s32[]{:T(128)} %constant.177.clone.1, s32[]{:T(128)} %constant.177.clone.1) | dynamic-update-slice | bytes 6148 | tf_op jit(solution)/shard_map/scatter-add | solution.py:75
  110.0 1.1 copy.282
  111.1 1.9 slice_add_fusion.2
  113.0 6.3 %scatter-add.30 = f32[16,3,16,256]{3,2,1,0:T(8,128)S(1)} dynamic-update-slice(f32[16,3,16,256]{3,2,1,0:T(8,128)S(1)} %scatter-add.29, f32[16,3,16,1]{3,2,1,0:T(8,128)} %slice_add_fusion.2, s32[]{:T(128)} %constant.177.clone.1, s32[]{:T(128)} %constant.177.clone.1, s32[]{:T(128)} %constant.177.clone.1, s32[]{:T(128)} %constant.181.clone.1) | dynamic-update-slice | bytes 6148 | tf_op jit(solution)/shard_map/scatter-add | solution.py:76
  119.3 2.2 reshape.294
  121.5 2.6 %copy.284 = f32[16,128,32]{2,1,0:T(8,128)} copy(f32[16,128,32]{2,0,1:T(8,128)} %bitcast.76) | data formatting | bytes 524288 | tf_op jit(solution)/shard_map/transpose | solution.py:100
  124.0 2.4 reshape.317
  126.4 2.9 %copy.285 = f32[4096,16]{1,0:T(8,128)} copy(f32[4096,16]{0,1:T(8,128)} %bitcast.77) | data formatting | bytes 524288 | tf_op jit(solution)/shard_map/reshape | solution.py:100
  129.3 30.2 %scatter_custom_fusion.2 = f32[16,12288]{0,1:T(8,128)} fusion(s32[4096]{0:T(1024)S(1)} %bitcast.87, f32[4096,16]{1,0:T(8,128)} %copy.285, f32[]{:T(128)} %constant.172.clone.1), kind=kCustom, calls=%fused_computation.3 | custom fusion | flops 65536 | bytes 786944 | tf_op jit(solution)/shard_map/scatter-add | solution.py:102
  159.5 5.3 %copy.294 = f32[16,3,16,256]{3,2,1,0:T(8,128)} copy(f32[16,3,16,256]{0,3,2,1:T(8,128)} %bitcast.75) | data formatting | bytes 1572864 | tf_op jit(solution)/shard_map/reshape | solution.py:103
  164.9 1.5 add_multiply_fusion.1
  166.4 1.0 slice.355
  167.4 2.4 collective-permute-start.2
  169.7 0.8 slice.364
  170.5 1.2 slice.354
  172.2 58.3 %psum.15 = bf16[16,2,256]{2,0,1:T(8,128)(2,1)S(1)} all-reduce(bf16[16,2,256]{2,0,1:T(8,128)(2,1)S(1)} %maximum_select_fusion.1), channel_id=1, replica_groups=mesh['face'=2,'rows'=16] {'rows'}, use_global_device_ids=true, to_apply=%region_6.7 | all-reduce | flops 8192 | bytes 32768 | tf_op jit(solution)/shard_map/psum | solution.py:9
  230.6 0.6 copy-done.4
  231.2 0.6 fusion.25
  231.8 1.3 copy.288
  233.1 2.2 pad_add_fusion
  235.4 0.8 pad_maximum_fusion.5
  236.2 1.3 collective-permute-start.3
  237.5 2.4 collective-permute-done.3
  240.1 2.3 scatter-add.34
  242.4 0.4 copy.290
  242.8 1.0 slice_add_fusion.1
  243.8 2.3 scatter-add.42
  246.1 0.4 copy.291
  246.5 1.2 slice_add_fusion
  247.6 5.5 %scatter-add.43 = f32[16,3,16,256]{3,2,1,0:T(8,128)} dynamic-update-slice(f32[16,3,16,256]{3,2,1,0:T(8,128)} %scatter-add.42, f32[16,3,16,1]{3,2,1,0:T(8,128)S(1)} %slice_add_fusion, s32[]{:T(128)} %constant.177.clone.1, s32[]{:T(128)} %constant.177.clone.1, s32[]{:T(128)} %constant.177.clone.1, s32[]{:T(128)} %constant.181.clone.1) | dynamic-update-slice | bytes 6148 | tf_op jit(solution)/shard_map/scatter-add | solution.py:76
  (60 shorter events, 2.5 us)
Async XLA Ops:
  0.0 82.2 %copy-start = (bf16[1,64,16,512]{3,2,1,0:T(8,128)(2,1)S(1)}, bf16[1,64,16,512]{3,2,1,0:T(8,128)(2,1)}, u32[]{:S(2)}) copy-start(bf16[1,64,16,512]{3,2,1,0:T(8,128)(2,1)} %param.22) | copy-start | bytes 3145732
  0.0 82.4 %copy-start.2 = (f32[16,3,16,256]{3,2,1,0:T(8,128)S(1)}, f32[16,3,16,256]{3,2,1,0:T(8,128)}, u32[]{:S(2)}) copy-start(f32[16,3,16,256]{3,2,1,0:T(8,128)} %param.21) | copy-start | bytes 2359300
  0.0 82.4 %copy-start.1 = (f32[16,3,16,256]{3,2,1,0:T(8,128)S(1)}, f32[16,3,16,256]{3,2,1,0:T(8,128)}, u32[]{:S(2)}) copy-start(f32[16,3,16,256]{3,2,1,0:T(8,128)} %param.20) | copy-start | bytes 2359300
  0.0 22.0 %copy-start.5 = (bf16[1,64,16]{1,2,0:T(8,128)(2,1)S(1)}, bf16[1,64,16]{1,2,0:T(8,128)(2,1)}, u32[]{:S(2)}) copy-start(bf16[1,64,16]{1,2,0:T(8,128)(2,1)} %param.23) | copy-start | bytes 6148
  3.3 17.5 %copy-start.6 = (s32[64]{0:T(128)}, s32[64]{0:T(128)S(1)}, u32[]{:S(2)}) copy-start(s32[64]{0:T(128)S(1)} %fusion.27) | copy-start | bytes 772
  4.8 84.0 %all-to-all-start = ((s32[16,1,256]{2,1,0:T(1,128)}), s32[16,1,256]{2,1,0:T(1,128)}, u32[]{:S(2)}, u32[]{:S(2)}) async-start(s32[16,1,256]{2,1,0:T(1,128)} %reshape.332), calls=%async_computation | async-start | bytes 32768 | tf_op jit(solution)/shard_map/all_to_all | solution.py:93
  14.8 80.2 %collective-permute-start = (f32[16,3,256]{2,0,1:T(8,128)}, f32[16,3,256]{2,0,1:T(8,128)}, u32[]{:S(2)}, u32[]{:S(2)}) collective-permute-start(f32[16,3,256]{2,0,1:T(8,128)} %bitcast.72), channel_id=1, source_target_pairs={{0,15},{1,0},{2,1},{3,2},{4,3},{5,4},{6,5},{7,6},{8,7},{9,8},{10,9... | collective-permute-start | bytes 147464 | tf_op jit(solution)/shard_map/ppermute | solution.py:24
  88.7 30.5 %all-to-all-start.1 = ((f32[16,8,512]{2,1,0:T(8,128)}), f32[16,8,512]{2,1,0:T(8,128)}, u32[]{:S(2)}, u32[]{:S(2)}) async-start(f32[16,8,512]{2,1,0:T(8,128)} %bitcast.78), calls=%async_computation.1 | async-start | bytes 524288 | tf_op jit(solution)/shard_map/all_to_all | solution.py:97
  96.5 3.7 %collective-permute-start.1 = (bf16[16,288]{1,0:T(8,128)(2,1)S(1)}, bf16[16,288]{1,0:T(8,128)(2,1)S(1)}, u32[]{:S(2)}, u32[]{:S(2)}) collective-permute-start(bf16[16,288]{1,0:T(8,128)(2,1)S(1)} %pad_maximum_fusion.4), channel_id=1, source_target_pairs={{0,16},{16,0},{1,17},{17,1},{2,18},{18,2},{3,19},{19,3},{4,20},{20... | collective-permute-start | bytes 27656 | tf_op jit(solution)/shard_map/ppermute | solution.py:19
  167.4 68.0 %collective-permute-start.2 = (f32[16,3,256]{2,0,1:T(8,128)S(1)}, f32[16,3,256]{2,0,1:T(8,128)S(1)}, u32[]{:S(2)}, u32[]{:S(2)}) collective-permute-start(f32[16,3,256]{2,0,1:T(8,128)S(1)} %bitcast.81), channel_id=1, source_target_pairs={{0,15},{1,0},{2,1},{3,2},{4,3},{5,4},{6,5},{7,6},{8,7},{9,8},{10,9... | collective-permute-start | bytes 147464 | tf_op jit(solution)/shard_map/ppermute | solution.py:24
  230.6 0.6 copy-start.4
  231.8 10.6 %slice-start = ((f32[16,2,16]{2,0,1:T(8,128)}), f32[16,1,16]{2,0,1:T(8,128)S(1)}, s32[]{:S(2)}) async-start(f32[16,2,16]{2,0,1:T(8,128)} %copy-done.4), calls=%async_computation.2 | async-start | bytes 16384 | tf_op jit(solution)/shard_map/slice | solution.py:63
  235.3 4.7 %copy-start.3 = (f32[16,3,16,256]{3,2,1,0:T(8,128)}, f32[16,3,16,256]{3,2,1,0:T(8,128)S(1)}, u32[]{:S(2)}) copy-start(f32[16,3,16,256]{3,2,1,0:T(8,128)S(1)} %pad_add_fusion) | copy-start | bytes 2359300
  236.2 3.7 %collective-permute-start.3 = (bf16[16,288]{1,0:T(8,128)(2,1)S(1)}, bf16[16,288]{1,0:T(8,128)(2,1)S(1)}, u32[]{:S(2)}, u32[]{:S(2)}) collective-permute-start(bf16[16,288]{1,0:T(8,128)(2,1)S(1)} %pad_maximum_fusion.5), channel_id=1, source_target_pairs={{0,16},{16,0},{1,17},{17,1},{2,18},{18,2},{3,19},{19,3},{4,20},{20... | collective-permute-start | bytes 27656 | tf_op jit(solution)/shard_map/ppermute | solution.py:19
where the time goes:
time: 255 us; the launch traced here: 253 us
  blocking collectives  116 us (45%)
  local copies, waits for them, and re-layouts  60.3 us (24%)
  other arithmetic  51.1 us (20%)
  starting transfers between devices  21.2 us (8%)
  waiting for transfers between devices  3.83 us (2%)
    psum x2, blocking collectives, broadcast(): return lax.psum(kept, axis)  116 us
    scatter-add x1, other arithmetic, ray_forcing(): jnp.zeros((levels, total), jnp.float32).at[:, cell_got.reshape(-1)]  30.2 us
    scatter-add x2, local copies, waits for them, and re-layouts, transpose_step(): result = result.at[:, :, :, edge - 1].add(right_col)  11.8 us
    all_to_all x1, starting transfers between devices, ray_forcing(): lax.all_to_all(cell_buf, 'rows', split_axis=0, concat_axis=0, tiled=True)  7.47 us
    ppermute x2, starting transfers between devices, shifted(): lax.ppermute(value, axis, [(i, (i + by) % count) for i in range(count)])  6.66 us
    reshape x1, local copies, waits for them, and re-layouts, ray_forcing(): return flat.reshape(field_shape)  5.31 us
    reshape x2, local copies, waits for them, and re-layouts, ray_forcing(): jnp.transpose(sums.reshape(-1, levels, width), (1, 0, 2))  5.31 us
    scatter-add x2, local copies, waits for them, and re-layouts, transpose_step(): result = result.at[:, :, :, 0].add(col_add)  5.29 us
  transfers between devices with their start and end apart: 6, of which 2 were waited for; matrix products, arithmetic and copies ran while one was open for 17% of the time, Pallas kernels for 0%

commit v1 on v0

--- a/solution.py
+++ b/solution.py
@@ -6,7 +6,7 @@
 
 def broadcast(value, axis, source):
     kept = jnp.where(lax.axis_index(axis) == source, value, 0).astype(value.dtype)
-    return lax.psum(kept, axis)
+    return jnp.sum(jax.lax.all_gather(kept, axis), 0)
 
 
 def from_partner(block, axis, apart):

time: 255 us -> 178 us (0.70)
  blocking collectives: 116 us -> 38.4 us
    psum x2 -> x0, blocking collectives: 116 us -> none  [broadcast(): return lax.psum(kept, axis)]
    all_gather x0 -> x2, blocking collectives: none -> 38.4 us  [broadcast(): return jnp.sum(jax.lax.all_gather(kept, axis), 0)]
  transfers between devices with their start and end apart: 6 -> 6, of which waited for: 2 -> 2; matrix products, arithmetic and copies ran while one was open for 17% -> 26% of each run, Pallas kernels for 0% -> 0%
where the time goes in v1:
time: 178 us; the launch traced here: 176 us
  local copies, waits for them, and re-layouts  60.3 us (34%)
  other arithmetic  52.2 us (29%)
  blocking collectives  38.4 us (22%)
  starting transfers between devices  21.2 us (12%)
  waiting for transfers between devices  3.83 us (2%)
    all_gather x2, blocking collectives, broadcast(): return jnp.sum(jax.lax.all_gather(kept, axis), 0)  38.4 us
    scatter-add x1, other arithmetic, ray_forcing(): jnp.zeros((levels, total), jnp.float32).at[:, cell_got.reshape(-1)]  30.2 us
    scatter-add x2, local copies, waits for them, and re-layouts, transpose_step(): result = result.at[:, :, :, edge - 1].add(right_col)  11.8 us
    all_to_all x1, starting transfers between devices, ray_forcing(): lax.all_to_all(cell_buf, 'rows', split_axis=0, concat_axis=0, tiled=True)  7.47 us
    ppermute x2, starting transfers between devices, shifted(): lax.ppermute(value, axis, [(i, (i + by) % count) for i in range(count)])  6.66 us
    reshape x1, local copies, waits for them, and re-layouts, ray_forcing(): return flat.reshape(field_shape)  5.31 us
    reshape x2, local copies, waits for them, and re-layouts, ray_forcing(): jnp.transpose(sums.reshape(-1, levels, width), (1, 0, 2))  5.31 us
    scatter-add x2, local copies, waits for them, and re-layouts, transpose_step(): result = result.at[:, :, :, 0].add(col_add)  5.29 us
  transfers between devices with their start and end apart: 6, of which 2 were waited for; matrix products, arithmetic and copies ran while one was open for 26% of the time, Pallas kernels for 0%

profile of v1, /device:TPU:0, one launch (start us, length us, event | category | flops | bytes accessed | tf_op | source)
XLA Modules:
  0.0 176.5 jit_solution(10021456218813422920)
XLA Ops:
  0.0 1.0 copy.242
  1.0 0.7 fusion.16
  1.8 0.8 select_reduce_fusion
  2.6 0.7 fusion.31
  3.3 0.8 scatter_custom_fusion
  4.1 0.7 reshape.400
  4.8 7.5 %all-to-all-start = ((s32[16,1,256]{2,1,0:T(1,128)}), s32[16,1,256]{2,1,0:T(1,128)}, u32[]{:S(2)}, u32[]{:S(2)}) async-start(s32[16,1,256]{2,1,0:T(1,128)} %reshape.400), calls=%async_computation | async-start | bytes 32768 | tf_op jit(solution)/shard_map/all_to_all | solution.py:93
  12.2 1.9 %fusion.32 = (f32[16,3,16,256]{3,2,1,0:T(8,128)S(1)}, f32[16,3,16,256]{3,2,1,0:T(8,128)S(1)}) fusion(f32[16,3,16,256]{3,2,1,0:T(8,128)} %param.20, f32[16,3,16,256]{3,2,1,0:T(8,128)} %param.19, f32[16,3,16,256]{3,2,1,0:T(8,128)} %param.21), kind=kLoop, calls=%fused_computation.85 | loop fusion | flops 393216 | bytes 3932160 | tf_op jit(solution)/shard_map/mul | solution.py:41
  14.1 0.6 copy.263
  14.8 4.3 %collective-permute-start = (f32[16,3,256]{2,0,1:T(8,128)}, f32[16,3,256]{2,0,1:T(8,128)}, u32[]{:S(2)}, u32[]{:S(2)}) collective-permute-start(f32[16,3,256]{2,0,1:T(8,128)} %bitcast.80), channel_id=1, source_target_pairs={{0,15},{1,0},{2,1},{3,2},{4,3},{5,4},{6,5},{7,6},{8,7},{9,8},{10,9... | collective-permute-start | bytes 147464 | tf_op jit(solution)/shard_map/ppermute | solution.py:24
  19.1 1.0 slice.335
  20.0 0.8 fusion.36
  20.8 1.2 slice.334
  22.6 18.4 %all_gather.8 = bf16[16,16,2,256]{3,1,2,0:T(8,128)(2,1)S(1)} all-gather(bf16[1,16,2,256]{3,1,2,0:T(8,128)(2,1)S(1)} %maximum_select_fusion), channel_id=1, replica_groups=mesh['face'=2,'rows'=16] {'rows'}, dimensions={0}, use_global_device_ids=true | all-gather | bytes 278528 | tf_op jit(solution)/shard_map/all_gather | solution.py:9
  41.1 0.6 fusion.27
  41.7 0.9 copy.238
  43.0 2.1 %pad_add_fusion.1 = f32[16,3,16,256]{3,2,1,0:T(8,128)S(1)} fusion(f32[16,3,15,256]{3,2,1,0:T(8,128)} %slice.335, f32[16,3,16,255]{3,2,1,0:T(8,128)} %slice.334, f32[16,3,16,256]{3,2,1,0:T(8,128)} %param.19, f32[16,3,16,256]{3,2,1,0:T(8,128)S(1)} %copy-done.2, f32[16,3,16,256]{3,2,1,0:T(8,128)S(1)} %copy-done.1), kind=kLoop, calls=%fused_computation.8 | loop fusion | flops 983040 | bytes 4666368 | tf_op jit(solution)/shard_map/add | solution.py:45
  45.0 1.3 fusion.28
  46.3 0.6 slice.350
  46.9 0.7 slice.352
  47.6 1.6 scatter_custom_fusion.1
  49.2 4.2 %all-to-all-start.1 = ((f32[16,8,512]{2,1,0:T(8,128)}), f32[16,8,512]{2,1,0:T(8,128)}, u32[]{:S(2)}, u32[]{:S(2)}) async-start(f32[16,8,512]{2,1,0:T(8,128)} %bitcast.86), calls=%async_computation.1 | async-start | bytes 524288 | tf_op jit(solution)/shard_map/all_to_all | solution.py:97
  53.4 0.5 broadcast.230
  53.9 1.3 reduce.14
  55.5 0.7 fusion.25
  56.2 0.8 pad_maximum_fusion.4
  57.0 1.5 collective-permute-start.1
  58.5 0.7 fusion.35
  59.2 1.5 collective-permute-done.1
  60.8 0.8 fusion.11
  61.7 2.1 %scatter-add.26 = f32[16,3,16,256]{3,2,1,0:T(8,128)S(1)} dynamic-update-slice(f32[16,3,16,256]{3,2,1,0:T(8,128)S(1)} %pad_add_fusion.1, f32[16,3,1,256]{3,2,1,0:T(1,128)S(1)} %slice_add_fusion.5, s32[]{:T(128)} %constant.180.clone.1, s32[]{:T(128)} %constant.180.clone.1, s32[]{:T(128)} %constant.177.clone.1, s32[]{:T(128)} %constant.180.clone.1) | dynamic-update-slice | bytes 98308 | tf_op jit(solution)/shard_map/scatter-add | solution.py:74
  63.8 0.7 maximum_bitcast_fusion
  64.5 1.1 copy.240
  65.6 1.8 %slice_add_fusion.3 = f32[16,3,16,1]{3,2,1,0:T(8,128)} fusion(f32[16,3,16,1]{3,2,1,0:T(8,128)} %copy.240, f32[16,3,16,256]{3,2,1,0:T(8,128)S(1)} %scatter-add.26), kind=kLoop, calls=%fused_computation.13 | loop fusion | flops 768 | bytes 9216 | tf_op jit(solution)/shard_map/add | solution.py:75
  67.4 3.0 %scatter-add.29 = f32[16,3,16,256]{3,2,1,0:T(8,128)S(1)} dynamic-update-slice(f32[16,3,16,256]{3,2,1,0:T(8,128)S(1)} %scatter-add.26, f32[16,3,16,1]{3,2,1,0:T(8,128)} %slice_add_fusion.3, s32[]{:T(128)} %constant.180.clone.1, s32[]{:T(128)} %constant.180.clone.1, s32[]{:T(128)} %constant.180.clone.1, s32[]{:T(128)} %constant.180.clone.1) | dynamic-update-slice | bytes 6148 | tf_op jit(solution)/shard_map/scatter-add | solution.py:75
  70.4 1.1 copy.241
  71.5 1.9 %slice_add_fusion.2 = f32[16,3,16,1]{3,2,1,0:T(8,128)} fusion(f32[16,3,16,1]{3,2,1,0:T(8,128)} %copy.241, f32[16,3,16,256]{3,2,1,0:T(8,128)S(1)} %scatter-add.29), kind=kLoop, calls=%fused_computation.12 | loop fusion | flops 768 | bytes 9216 | tf_op jit(solution)/shard_map/add | solution.py:76
  73.5 6.3 %scatter-add.30 = f32[16,3,16,256]{3,2,1,0:T(8,128)S(1)} dynamic-update-slice(f32[16,3,16,256]{3,2,1,0:T(8,128)S(1)} %scatter-add.29, f32[16,3,16,1]{3,2,1,0:T(8,128)} %slice_add_fusion.2, s32[]{:T(128)} %constant.180.clone.1, s32[]{:T(128)} %constant.180.clone.1, s32[]{:T(128)} %constant.180.clone.1, s32[]{:T(128)} %constant.184.clone.1) | dynamic-update-slice | bytes 6148 | tf_op jit(solution)/shard_map/scatter-add | solution.py:76
  79.8 2.2 %reshape.362 = f32[128,16,32]{2,1,0:T(8,128)} reshape(f32[16,8,512]{2,1,0:T(8,128)} %all-to-all-done.1) | data formatting | bytes 524288 | tf_op jit(solution)/shard_map/reshape | solution.py:100
  82.0 2.6 %copy.243 = f32[16,128,32]{2,1,0:T(8,128)} copy(f32[16,128,32]{2,0,1:T(8,128)} %bitcast.84) | data formatting | bytes 524288 | tf_op jit(solution)/shard_map/transpose | solution.py:100
  84.5 2.4 %reshape.385 = f32[16,4096]{1,0:T(8,128)} reshape(f32[16,128,32]{2,1,0:T(8,128)} %copy.243) | data formatting | bytes 524288 | tf_op jit(solution)/shard_map/reshape | solution.py:100
  86.9 2.9 %copy.244 = f32[4096,16]{1,0:T(8,128)} copy(f32[4096,16]{0,1:T(8,128)} %bitcast.85) | data formatting | bytes 524288 | tf_op jit(solution)/shard_map/reshape | solution.py:100
  89.8 30.2 %scatter_custom_fusion.2 = f32[16,12288]{0,1:T(8,128)} fusion(s32[4096]{0:T(1024)S(1)} %bitcast.95, f32[4096,16]{1,0:T(8,128)} %copy.244, f32[]{:T(128)} %constant.175.clone.1), kind=kCustom, calls=%fused_computation.3 | custom fusion | flops 65536 | bytes 786944 | tf_op jit(solution)/shard_map/scatter-add | solution.py:102
  120.0 5.3 %copy.253 = f32[16,3,16,256]{3,2,1,0:T(8,128)} copy(f32[16,3,16,256]{0,3,2,1:T(8,128)} %bitcast.83) | data formatting | bytes 1572864 | tf_op jit(solution)/shard_map/reshape | solution.py:103
  125.4 1.5 add_multiply_fusion.1
  126.9 1.0 slice.355
  127.9 2.4 %collective-permute-start.2 = (f32[16,3,256]{2,0,1:T(8,128)S(1)}, f32[16,3,256]{2,0,1:T(8,128)S(1)}, u32[]{:S(2)}, u32[]{:S(2)}) collective-permute-start(f32[16,3,256]{2,0,1:T(8,128)S(1)} %bitcast.89), channel_id=1, source_target_pairs={{0,15},{1,0},{2,1},{3,2},{4,3},{5,4},{6,5},{7,6},{8,7},{9,8},{10,9... | collective-permute-start | bytes 147464 | tf_op jit(solution)/shard_map/ppermute | solution.py:24
  130.2 0.8 slice.364
  131.0 1.2 slice.354
  132.7 20.1 %all_gather.9 = bf16[16,16,2,256]{3,1,2,0:T(8,128)(2,1)} all-gather(bf16[1,16,2,256]{3,1,2,0:T(8,128)(2,1)S(1)} %maximum_select_fusion.1), channel_id=1, replica_groups=mesh['face'=2,'rows'=16] {'rows'}, dimensions={0}, use_global_device_ids=true | all-gather | bytes 278528 | tf_op jit(solution)/shard_map/all_gather | solution.py:9
  152.8 1.0 reduce_sum.35
  153.9 0.6 copy-done.4
  154.5 0.6 fusion.29
  155.1 1.3 copy.247
  156.4 2.2 %pad_add_fusion = f32[16,3,16,256]{3,2,1,0:T(8,128)S(1)} fusion(f32[16,3,15,256]{3,2,1,0:T(8,128)} %slice.355, f32[16,3,16,255]{3,2,1,0:T(8,128)} %slice.354, f32[16,3,16,256]{3,2,1,0:T(8,128)S(1)} %copy-done.2, f32[16,3,16,256]{3,2,1,0:T(8,128)S(1)} %copy-done.1, f32[16,3,16,256]{3,2,1,0:T(8,128)S(1)} %scatter-add.30, f32[16,3,16,256]{3,2,1,0:T(8,128)} %copy.253), kind=kLoop, calls=%fused_computation.7 | loop fusion | flops 1179648 | bytes 5452800 | tf_op jit(solution)/shard_map/add | solution.py:45
  158.7 0.8 pad_maximum_fusion.5
  159.4 1.3 collective-permute-start.3
  160.8 2.4 %collective-permute-done.3 = bf16[16,288]{1,0:T(8,128)(2,1)S(1)} collective-permute-done((bf16[16,288]{1,0:T(8,128)(2,1)S(1)}, bf16[16,288]{1,0:T(8,128)(2,1)S(1)}, u32[]{:S(2)}, u32[]{:S(2)}) %collective-permute-start.3) | collective-permute-done | bytes 9248 | tf_op jit(solution)/shard_map/ppermute | solution.py:19
  163.4 2.3 %scatter-add.34 = f32[16,3,16,256]{3,2,1,0:T(8,128)} dynamic-update-slice(f32[16,3,16,256]{3,2,1,0:T(8,128)} %copy-done.3, f32[16,3,1,256]{3,2,1,0:T(1,128)S(1)} %slice_add_fusion.4, s32[]{:T(128)} %constant.180.clone.1, s32[]{:T(128)} %constant.180.clone.1, s32[]{:T(128)} %constant.177.clone.1, s32[]{:T(128)} %constant.180.clone.1) | dynamic-update-slice | bytes 98308 | tf_op jit(solution)/shard_map/scatter-add | solution.py:74
  166.0 1.0 slice_add_fusion.1
  167.1 2.3 %scatter-add.42 = f32[16,3,16,256]{3,2,1,0:T(8,128)} dynamic-update-slice(f32[16,3,16,256]{3,2,1,0:T(8,128)} %scatter-add.34, f32[16,3,16,1]{3,2,1,0:T(8,128)S(1)} %slice_add_fusion.1, s32[]{:T(128)} %constant.180.clone.1, s32[]{:T(128)} %constant.180.clone.1, s32[]{:T(128)} %constant.180.clone.1, s32[]{:T(128)} %constant.180.clone.1) | dynamic-update-slice | bytes 6148 | tf_op jit(solution)/shard_map/scatter-add | solution.py:75
  169.4 0.4 copy.250
  169.7 1.2 slice_add_fusion
  170.9 5.5 %scatter-add.43 = f32[16,3,16,256]{3,2,1,0:T(8,128)} dynamic-update-slice(f32[16,3,16,256]{3,2,1,0:T(8,128)} %scatter-add.42, f32[16,3,16,1]{3,2,1,0:T(8,128)S(1)} %slice_add_fusion, s32[]{:T(128)} %constant.180.clone.1, s32[]{:T(128)} %constant.180.clone.1, s32[]{:T(128)} %constant.180.clone.1, s32[]{:T(128)} %constant.184.clone.1) | dynamic-update-slice | bytes 6148 | tf_op jit(solution)/shard_map/scatter-add | solution.py:76
  (62 shorter events, 3.0 us)
Async XLA Ops:
  0.0 42.7 %copy-start = (bf16[1,64,16,512]{3,2,1,0:T(8,128)(2,1)S(1)}, bf16[1,64,16,512]{3,2,1,0:T(8,128)(2,1)}, u32[]{:S(2)}) copy-start(bf16[1,64,16,512]{3,2,1,0:T(8,128)(2,1)} %param.22) | copy-start | bytes 3145732
  0.0 42.9 %copy-start.2 = (f32[16,3,16,256]{3,2,1,0:T(8,128)S(1)}, f32[16,3,16,256]{3,2,1,0:T(8,128)}, u32[]{:S(2)}) copy-start(f32[16,3,16,256]{3,2,1,0:T(8,128)} %param.21) | copy-start | bytes 2359300
  0.0 42.9 %copy-start.1 = (f32[16,3,16,256]{3,2,1,0:T(8,128)S(1)}, f32[16,3,16,256]{3,2,1,0:T(8,128)}, u32[]{:S(2)}) copy-start(f32[16,3,16,256]{3,2,1,0:T(8,128)} %param.20) | copy-start | bytes 2359300
  0.0 22.0 %copy-start.5 = (bf16[1,64,16]{1,2,0:T(8,128)(2,1)S(1)}, bf16[1,64,16]{1,2,0:T(8,128)(2,1)}, u32[]{:S(2)}) copy-start(bf16[1,64,16]{1,2,0:T(8,128)(2,1)} %param.23) | copy-start | bytes 6148
  3.3 17.5 %copy-start.6 = (s32[64]{0:T(128)}, s32[64]{0:T(128)S(1)}, u32[]{:S(2)}) copy-start(s32[64]{0:T(128)S(1)} %fusion.31) | copy-start | bytes 772
  4.8 44.5 %all-to-all-start = ((s32[16,1,256]{2,1,0:T(1,128)}), s32[16,1,256]{2,1,0:T(1,128)}, u32[]{:S(2)}, u32[]{:S(2)}) async-start(s32[16,1,256]{2,1,0:T(1,128)} %reshape.400), calls=%async_computation | async-start | bytes 32768 | tf_op jit(solution)/shard_map/all_to_all | solution.py:93
  14.8 40.7 %collective-permute-start = (f32[16,3,256]{2,0,1:T(8,128)}, f32[16,3,256]{2,0,1:T(8,128)}, u32[]{:S(2)}, u32[]{:S(2)}) collective-permute-start(f32[16,3,256]{2,0,1:T(8,128)} %bitcast.80), channel_id=1, source_target_pairs={{0,15},{1,0},{2,1},{3,2},{4,3},{5,4},{6,5},{7,6},{8,7},{9,8},{10,9... | collective-permute-start | bytes 147464 | tf_op jit(solution)/shard_map/ppermute | solution.py:24
  49.2 30.5 %all-to-all-start.1 = ((f32[16,8,512]{2,1,0:T(8,128)}), f32[16,8,512]{2,1,0:T(8,128)}, u32[]{:S(2)}, u32[]{:S(2)}) async-start(f32[16,8,512]{2,1,0:T(8,128)} %bitcast.86), calls=%async_computation.1 | async-start | bytes 524288 | tf_op jit(solution)/shard_map/all_to_all | solution.py:97
  57.0 3.7 %collective-permute-start.1 = (bf16[16,288]{1,0:T(8,128)(2,1)S(1)}, bf16[16,288]{1,0:T(8,128)(2,1)S(1)}, u32[]{:S(2)}, u32[]{:S(2)}) collective-permute-start(bf16[16,288]{1,0:T(8,128)(2,1)S(1)} %pad_maximum_fusion.4), channel_id=1, source_target_pairs={{0,16},{16,0},{1,17},{17,1},{2,18},{18,2},{3,19},{19,3},{4,20},{20... | collective-permute-start | bytes 27656 | tf_op jit(solution)/shard_map/ppermute | solution.py:19
  127.9 30.8 %collective-permute-start.2 = (f32[16,3,256]{2,0,1:T(8,128)S(1)}, f32[16,3,256]{2,0,1:T(8,128)S(1)}, u32[]{:S(2)}, u32[]{:S(2)}) collective-permute-start(f32[16,3,256]{2,0,1:T(8,128)S(1)} %bitcast.89), channel_id=1, source_target_pairs={{0,15},{1,0},{2,1},{3,2},{4,3},{5,4},{6,5},{7,6},{8,7},{9,8},{10,9... | collective-permute-start | bytes 147464 | tf_op jit(solution)/shard_map/ppermute | solution.py:24
  153.9 0.6 copy-start.4
  155.1 10.6 %slice-start = ((f32[16,2,16]{2,0,1:T(8,128)}), f32[16,1,16]{2,0,1:T(8,128)S(1)}, s32[]{:S(2)}) async-start(f32[16,2,16]{2,0,1:T(8,128)} %copy-done.4), calls=%async_computation.2 | async-start | bytes 16384 | tf_op jit(solution)/shard_map/slice | solution.py:63
  158.6 4.7 %copy-start.3 = (f32[16,3,16,256]{3,2,1,0:T(8,128)}, f32[16,3,16,256]{3,2,1,0:T(8,128)S(1)}, u32[]{:S(2)}) copy-start(f32[16,3,16,256]{3,2,1,0:T(8,128)S(1)} %pad_add_fusion) | copy-start | bytes 2359300
  159.4 3.7 %collective-permute-start.3 = (bf16[16,288]{1,0:T(8,128)(2,1)S(1)}, bf16[16,288]{1,0:T(8,128)(2,1)S(1)}, u32[]{:S(2)}, u32[]{:S(2)}) collective-permute-start(bf16[16,288]{1,0:T(8,128)(2,1)S(1)} %pad_maximum_fusion.5), channel_id=1, source_target_pairs={{0,16},{16,0},{1,17},{17,1},{2,18},{18,2},{3,19},{19,3},{4,20},{20... | collective-permute-start | bytes 27656 | tf_op jit(solution)/shard_map/ppermute | solution.py:19
